TPU v7x, 32 devices: a whole 2x2x4 slice. The times are simulated.
32 devices in a mesh: groups: 2 (over y), blk: 4 (over z), col: 4 (over x, core).
Axes of the slice: x: 2, y: 2, z: 4, core: 2. Of those that a mesh axis runs over, the one named last changes fastest.
Arguments:
- aic: float32 [256, 32768], P(('groups', 'blk'), 'col'), parts along dimension 0, may hold values from -0.03125 to 0.03125
- downwash: float32 [8, 8192, 384], P(('groups', 'col'), 'blk'), parts along dimension 0, may hold values from -6 to 6
- node_modes: float32 [6, 32, 192], P(None, 'blk'), may hold values from -0.4375 to 0.4375
- src_rows: int32 [4, 4, 4, 8], P('blk', 'col'), may hold values from 0 to 7
- dst_nodes: int32 [4, 4, 4, 8], P('blk', 'col'), may hold values from 0 to 7
- counts: int32 [4, 4, 4], P('blk', 'col'), may hold values from 0 to 8, as said below
- spline_weights: float32 [4, 4, 6, 4, 8], P('blk', 'col'), may hold values from -0.6 to 0.6
Outputs:
- gaf: float32 [384, 384], P('groups'), parts along dimension 0
There are 2 independent parts, one for each index of `groups`. A program takes and returns all parts, laid end to end along the dimension named above; an argument that names none is the same for every part. Nothing has to cross between parts.
Inputs may be any that keep to these rules, and one draw needn't show every extreme that they name: `counts`: slot s of a list is live when s < count; every source sub-block sends 8 live slots to its own owner, and one owner receives 8 live slots from every source sub-block. `src_rows`: rows within a sub-block of 8 rows. `dst_nodes`: nodes within an owner.
All inputs are finite; a program needn't handle non-finite values.
Results may differ from a plain program's by a relative error of at most 0.0003.
Values sent between devices are 32-bit elements; how exact they have to be, the bound alone decides.
A program may use at most 64 MiB of HBM per device.

v0:
```python
import jax
import jax.numpy as jnp
from jax import lax
from jax.sharding import PartitionSpec as P


def shifted(value, axis, steps):
    count = lax.axis_size(axis)
    pairs = [(source, (source + steps) % count) for source in range(count)]
    return lax.ppermute(value, axis, pairs)


def shards(aic, downwash, node_modes, src_rows, dst_nodes, counts, spline_weights):
    cycle_size = lax.axis_size("blk")
    col_count = lax.axis_size("col")
    device = lax.axis_index("blk")
    own_block = downwash[0]
    panel_rows = own_block.shape[0]

    def product(shapes, source):
        columns = lax.dynamic_slice_in_dim(aic, source * panel_rows, panel_rows, 1)
        return jnp.dot(
            columns, shapes, precision=lax.Precision.HIGHEST, preferred_element_type=jnp.float32
        )

    halfway = cycle_size // 2

    def advance(offset, running):
        pressure, forward, behind = running
        forward = shifted(forward, "blk", 1)
        behind = shifted(behind, "blk", -1)
        pressure = pressure + product(forward, (device - offset) % cycle_size)
        pressure = pressure + product(behind, (device + offset) % cycle_size)
        return (pressure, forward, behind)

    pressure = product(own_block, device)
    pressure, forward, behind = lax.fori_loop(1, halfway, advance, (pressure, own_block, own_block))
    forward = shifted(forward, "blk", 1)
    pressure = pressure + product(forward, (device - halfway) % cycle_size)
    slots = src_rows.shape[-1]
    slot_index = jnp.arange(slots, dtype=jnp.int32)
    all_rows, all_nodes, all_counts = (
        lax.all_gather(src_rows, "col", axis=1, tiled=True),
        lax.all_gather(dst_nodes, "col", axis=1, tiled=True),
        lax.all_gather(counts, "col", axis=1, tiled=True),
    )
    weight_all = lax.all_gather(spline_weights, "col", axis=1, tiled=True)
    sub_rows = pressure.shape[0] // col_count
    offsets = jnp.arange(col_count, dtype=jnp.int32)[:, None, None] * sub_rows
    shifted_rows = all_rows[0] + offsets
    row_ids = jnp.transpose(shifted_rows, (1, 0, 2)).reshape(cycle_size, col_count * slots)
    node_ids = jnp.transpose(all_nodes[0], (1, 0, 2)).reshape(cycle_size, col_count * slots)
    live_sub = (slot_index[None, None, :] < all_counts[0][:, :, None]).astype(jnp.float32)
    live = jnp.transpose(live_sub, (1, 0, 2)).reshape(cycle_size, col_count * slots)
    weight_rows = jnp.transpose(weight_all[0], (1, 2, 0, 3)).reshape(
        6, cycle_size, col_count * slots
    )
    node_count = node_modes.shape[1]
    forces = pressure[row_ids.T]
    picks = (node_ids[None, :, :] == jnp.arange(node_count, dtype=jnp.int32)[:, None, None]).astype(
        jnp.float32
    )
    spread = weight_rows[:, None, :, :] * live[None, None, :, :] * picks[None, :, :, :]
    spread = spread.reshape(6 * node_count, cycle_size, row_ids.shape[1])
    arrived_forces, arrived_spread = (
        lax.all_to_all(forces, "blk", split_axis=1, concat_axis=1, tiled=True),
        lax.all_to_all(spread, "blk", split_axis=1, concat_axis=1, tiled=True),
    )
    loads = jnp.einsum(
        "jsc,csk->jk", arrived_spread, arrived_forces, precision=lax.Precision.HIGHEST
    )
    flat_modes = node_modes.reshape(6 * node_count, node_modes.shape[2])
    modal = jnp.einsum("jm,jk->mk", flat_modes, loads, precision=lax.Precision.HIGHEST)
    return lax.psum(modal, ("blk", "col"))


def solution(mesh):
    placed = (
        P(("groups", "blk"), "col"),
        P(("groups", "col"), "blk", None),
        P(None, "blk", None),
        P("blk", "col", None, None),
        P("blk", "col", None, None),
        P("blk", "col", None),
        P("blk", "col", None, None, None),
    )
    return jax.shard_map(
        shards, mesh=mesh, in_specs=placed, out_specs=P("groups", None), check_vma=False
    )
```

profile of v0, /device:TPU:0, one launch (start us, length us, event | category | flops | bytes accessed | tf_op | source)
XLA Modules:
  0.0 330.8 jit_solution(2935997758581484725)
XLA Ops:
  6.5 3.1 collective-permute-start
  9.6 2.0 collective-permute-start.1
  11.6 69.3 %collective-permute-done = f32[2048,384]{1,0:T(8,128)} collective-permute-done((f32[2048,384]{1,0:T(8,128)}, f32[2048,384]{1,0:T(8,128)}, u32[]{:S(2)}, u32[]{:S(2)}) %collective-permute-start) | collective-permute-done | bytes 3145760 | tf_op jit(solution)/shard_map/while/body/eval_jaxpr/ppermute | solution.py:10
  80.9 5.2 %all_gather.13 = s32[1,4,4]{2,0,1:T(1,128)S(1)} all-gather(s32[1,1,4]{2,0,1:T(1,128)} %bitcast.57), channel_id=1, replica_groups=mesh['groups'=2,'blk'=4,'col'=4] {'col'}, dimensions={1}, use_global_device_ids=true | all-gather | bytes 80 | tf_op jit(solution)/shard_map/all_gather | solution.py:45
  86.1 5.3 %all_gather.14 = s32[1,4,4,8]{3,2,0,1:T(4,128)S(1)} all-gather(s32[1,1,4,8]{3,2,0,1:T(4,128)} %bitcast.55), channel_id=1, replica_groups=mesh['groups'=2,'blk'=4,'col'=4] {'col'}, dimensions={1}, use_global_device_ids=true | all-gather | bytes 640 | tf_op jit(solution)/shard_map/all_gather | solution.py:44
  91.5 5.4 %all_gather.12 = f32[1,4,6,4,8]{4,3,2,0,1:T(4,128)S(1)} all-gather(f32[1,1,6,4,8]{4,3,2,0,1:T(4,128)} %bitcast.53), channel_id=1, replica_groups=mesh['groups'=2,'blk'=4,'col'=4] {'col'}, dimensions={1}, use_global_device_ids=true | all-gather | bytes 3840 | tf_op jit(solution)/shard_map/all_gather | solution.py:47
  97.5 0.7 reshape.63
  98.3 69.4 %all-to-all-start = ((f32[4,1,1536]{2,1,0:T(1,128)}), f32[4,1,1536]{2,1,0:T(1,128)S(1)}, u32[]{:S(2)}, u32[]{:S(2)}) async-start(f32[4,1,1536]{2,1,0:T(1,128)} %reshape.63), calls=%async_computation | async-start | bytes 49152 | tf_op jit(solution)/shard_map/all_to_all | solution.py:67
  167.6 5.3 %all_gather.15 = s32[1,4,4,8]{3,2,0,1:T(4,128)S(1)} all-gather(s32[1,1,4,8]{3,2,0,1:T(4,128)} %bitcast.56), channel_id=1, replica_groups=mesh['groups'=2,'blk'=4,'col'=4] {'col'}, dimensions={1}, use_global_device_ids=true | all-gather | bytes 640 | tf_op jit(solution)/shard_map/all_gather | solution.py:43
  173.4 3.6 %fusion.3 = f32[32,384]{1,0:T(8,128)S(1)} fusion(f32[32,8192]{1,0:T(8,128)S(1)} %copy-done, s32[]{:T(128)S(6)} %select_n.35, f32[1,2048,384]{2,1,0:T(8,128)} %param.8), kind=kOutput, calls=%fused_computation.9 | convolution fusion | flops 301989888 | bytes 3457028 | tf_op jit(solution)/shard_map/dot_general | solution.py:22
  177.0 3.6 %convolution_add_fusion.2 = f32[32,384]{1,0:T(8,128)S(1)} fusion(f32[32,384]{1,0:T(8,128)S(1)} %fusion.3, f32[2048,384]{1,0:T(8,128)} %collective-permute-done, f32[32,8192]{1,0:T(8,128)S(1)} %copy-done, s32[]{:T(128)S(6)} %select_n.37), kind=kOutput, calls=%fused_computation.5 | convolution fusion | flops 302002176 | bytes 3506180 | tf_op jit(solution)/shard_map/while/body/eval_jaxpr/dot_general | solution.py:22
  180.7 3.6 %convolution_add_fusion.1 = f32[32,384]{1,0:T(8,128)S(1)} fusion(f32[32,384]{1,0:T(8,128)S(1)} %convolution_add_fusion.2, f32[2048,384]{1,0:T(8,128)} %collective-permute-done.1, f32[32,8192]{1,0:T(8,128)S(1)} %copy-done, s32[]{:T(128)S(6)} %select_n.39), kind=kOutput, calls=%fused_computation.4 | convolution fusion | flops 302002176 | bytes 3506180 | tf_op jit(solution)/shard_map/while/body/eval_jaxpr/dot_general | solution.py:22
  184.4 30.8 %collective-permute-done.2 = f32[2048,384]{1,0:T(8,128)} collective-permute-done((f32[2048,384]{1,0:T(8,128)}, f32[2048,384]{1,0:T(8,128)}, u32[]{:S(2)}, u32[]{:S(2)}) %collective-permute-start.2) | collective-permute-done | bytes 3145760 | tf_op jit(solution)/shard_map/ppermute | solution.py:10
  215.1 3.6 %convolution_add_fusion = f32[32,384]{1,0:T(8,128)S(1)} fusion(f32[32,384]{1,0:T(8,128)S(1)} %convolution_add_fusion.1, f32[2048,384]{1,0:T(8,128)} %collective-permute-done.2, f32[32,8192]{1,0:T(8,128)S(1)} %copy-done, s32[]{:T(128)S(6)} %select_n.41), kind=kOutput, calls=%fused_computation.3 | convolution fusion | flops 302002176 | bytes 3506180 | tf_op jit(solution)/shard_map/dot_general | solution.py:22
  218.8 0.8 gather_fusion
  219.6 0.7 copy.39
  220.3 3.4 %all-to-all-start.1 = ((f32[32,4,384]{2,0,1:T(8,128)}), f32[32,4,384]{2,0,1:T(8,128)S(1)}, u32[]{:S(2)}, u32[]{:S(2)}) async-start(f32[32,4,384]{2,0,1:T(8,128)} %copy.39), calls=%async_computation.1 | async-start | bytes 393216 | tf_op jit(solution)/shard_map/all_to_all | solution.py:66
  223.7 0.6 broadcast.44
  224.3 0.8 reduce
  225.2 4.7 %all-to-all-done.1 = f32[32,4,384]{2,0,1:T(8,128)S(1)} async-done(((f32[32,4,384]{2,0,1:T(8,128)}), f32[32,4,384]{2,0,1:T(8,128)S(1)}, u32[]{:S(2)}, u32[]{:S(2)}) %all-to-all-start.1) | async-done | bytes 196640 | tf_op jit(solution)/shard_map/all_to_all | solution.py:66
  229.9 0.3 convolution_bitcast_fusion.1
  230.2 1.2 convolution_bitcast_fusion
  231.4 90.9 %all-reduce.2.cloned.1.call-done = f32[192,384]{1,0:T(8,128)} async-done(((f32[192,384]{1,0:T(8,128)}), f32[192,384]{1,0:T(8,128)}) %all-reduce.2.cloned.1.call-update) | async-done | bytes 294928 | tf_op jit(solution)/shard_map/psum | solution.py:74
  322.3 1.7 copy.41
  (35 shorter events, 1.3 us)
Async XLA Ops:
  6.5 166.8 %copy-start = (f32[32,8192]{1,0:T(8,128)S(1)}, f32[32,8192]{1,0:T(8,128)}, u32[]{:S(2)}) copy-start(f32[32,8192]{1,0:T(8,128)} %param.7) | copy-start | bytes 3145732
  6.5 74.4 %collective-permute-start = (f32[2048,384]{1,0:T(8,128)}, f32[2048,384]{1,0:T(8,128)}, u32[]{:S(2)}, u32[]{:S(2)}) collective-permute-start(f32[2048,384]{1,0:T(8,128)} %bitcast.45), channel_id=1, source_target_pairs={{0,4},{4,8},{8,12},{12,0},{1,5},{5,9},{9,13},{13,1},{2,6},{6,10},{... | collective-permute-start | bytes 9437192 | tf_op jit(solution)/shard_map/while/body/eval_jaxpr/ppermute | solution.py:10
  9.6 171.1 %collective-permute-start.1 = (f32[2048,384]{1,0:T(8,128)}, f32[2048,384]{1,0:T(8,128)}, u32[]{:S(2)}, u32[]{:S(2)}) collective-permute-start(f32[2048,384]{1,0:T(8,128)} %bitcast.46), channel_id=1, source_target_pairs={{0,12},{4,0},{8,4},{12,8},{1,13},{5,1},{9,5},{13,9},{2,14},{6,2},{... | collective-permute-start | bytes 9437192 | tf_op jit(solution)/shard_map/while/body/eval_jaxpr/ppermute | solution.py:10
  80.9 134.2 %collective-permute-start.2 = (f32[2048,384]{1,0:T(8,128)}, f32[2048,384]{1,0:T(8,128)}, u32[]{:S(2)}, u32[]{:S(2)}) collective-permute-start(f32[2048,384]{1,0:T(8,128)} %collective-permute-done), channel_id=1, source_target_pairs={{0,4},{4,8},{8,12},{12,0},{1,5},{5,9},{9,13},{13,1},{2,6},{6,10},{... | collective-permute-start | bytes 9437192 | tf_op jit(solution)/shard_map/ppermute | solution.py:10
  98.3 122.0 %all-to-all-start = ((f32[4,1,1536]{2,1,0:T(1,128)}), f32[4,1,1536]{2,1,0:T(1,128)S(1)}, u32[]{:S(2)}, u32[]{:S(2)}) async-start(f32[4,1,1536]{2,1,0:T(1,128)} %reshape.63), calls=%async_computation | async-start | bytes 49152 | tf_op jit(solution)/shard_map/all_to_all | solution.py:67
  184.3 45.9 %copy-start.1 = (f32[6,8,192]{2,1,0:T(8,128)S(1)}, f32[6,8,192]{2,1,0:T(8,128)}, u32[]{:S(2)}) copy-start(f32[6,8,192]{2,1,0:T(8,128)} %param.9) | copy-start | bytes 110596
  220.3 9.6 %all-to-all-start.1 = ((f32[32,4,384]{2,0,1:T(8,128)}), f32[32,4,384]{2,0,1:T(8,128)S(1)}, u32[]{:S(2)}, u32[]{:S(2)}) async-start(f32[32,4,384]{2,0,1:T(8,128)} %copy.39), calls=%async_computation.1 | async-start | bytes 393216 | tf_op jit(solution)/shard_map/all_to_all | solution.py:66
  223.7 98.6 %all-reduce.2.cloned.1.call-start = ((), (), s32[]{:S(2)}) async-start(), calls=%async_computation.2 | async-start | bytes 589824 | tf_op jit(solution)/shard_map/psum | solution.py:74
Sparse Core Ops, SparseCore 0:
  231.5 90.7 all-reduce.1
where the time goes:
time: 331 us
  waiting for transfers between devices  196 us (59%)
  starting transfers between devices  77.9 us (24%)
  blocking collectives  21.2 us (6%)
  matrix products  16 us (5%)
  between operations  13.6 us (4%)
  local copies, waits for them, and re-layouts  5.54 us (2%)
    ppermute x3, waiting for transfers between devices, shifted(): return lax.ppermute(value, axis, pairs)  100 us
    psum x1, waiting for transfers between devices, shards(): return lax.psum(modal, ('blk', 'col'))  90.9 us
    all_to_all x1, starting transfers between devices, shards(): lax.all_to_all(spread, 'blk', split_axis=1, concat_axis=1, tiled=True)  69.4 us
    dot_general x4, matrix products, product(): jnp.dot(columns, shapes, precision=lax.Precision.HIGHEST, preferred_eleme...  14.6 us
  transfers between devices with their start and end apart: 6, of which 4 were waited for; matrix products, arithmetic and copies ran while one was open for 6% of the time, Pallas kernels for 0%

commit v1 on v0

--- a/solution.py
+++ b/solution.py
@@ -2,6 +2,9 @@
 import jax.numpy as jnp
 from jax import lax
 from jax.sharding import PartitionSpec as P
+
+
+HIGHEST = lax.Precision.HIGHEST
 
 
 def shifted(value, axis, steps):
@@ -10,7 +13,7 @@
     return lax.ppermute(value, axis, pairs)
 
 
-def shards(aic, downwash, node_modes, src_rows, dst_nodes, counts, spline_weights):
+def by_rotation(aic, downwash, node_modes, src_rows, dst_nodes, counts, spline_weights):
     cycle_size = lax.axis_size("blk")
     col_count = lax.axis_size("col")
     device = lax.axis_index("blk")
@@ -74,6 +77,32 @@
     return lax.psum(modal, ("blk", "col"))
 
 
+def by_collectives(aic, downwash, node_modes, src_rows, dst_nodes, counts, spline_weights):
+    blocks = lax.axis_size("blk")
+    col_count = lax.axis_size("col")
+    dofs, node_count, modes = node_modes.shape
+    slots = src_rows.shape[-1]
+    rows = aic.shape[0]
+    sub_rows = rows // col_count
+    mine = lax.all_to_all(aic, "blk", split_axis=1, concat_axis=0, tiled=True)
+    live = jnp.arange(slots, dtype=jnp.int32) < counts[0, 0][:, None]
+    row_pick = src_rows[0, 0][..., None] == jnp.arange(sub_rows, dtype=jnp.int32)
+    node_pick = dst_nodes[0, 0][..., None] == jnp.arange(node_count, dtype=jnp.int32)
+    row_pick = jnp.where(live[..., None], row_pick.astype(jnp.float32), 0.0)
+    weighted = spline_weights[0, 0][..., None] * node_pick.astype(jnp.float32)
+    spline = jnp.einsum("osr,dosn->rdon", row_pick, weighted, precision=HIGHEST)
+    spline = lax.all_gather(spline, ("blk", "col"), axis=0, tiled=True)
+    every_mode = lax.all_gather(node_modes, "blk", axis=1, tiled=True)
+    force = jnp.dot(
+        spline.reshape(blocks * rows, dofs * blocks * node_count),
+        every_mode.reshape(dofs * blocks * node_count, modes),
+        precision=HIGHEST,
+    )
+    pressure = jnp.dot(mine, downwash[0], precision=HIGHEST, preferred_element_type=jnp.float32)
+    part = lax.dot_general(force, pressure, (((0,), (0,)), ((), ())), precision=HIGHEST)
+    return lax.psum(part, ("blk", "col"))
+
+
 def solution(mesh):
     placed = (
         P(("groups", "blk"), "col"),
@@ -84,6 +113,14 @@
         P("blk", "col", None),
         P("blk", "col", None, None, None),
     )
+
+    def shards(*operands):
+        aic, node_modes = operands[0], operands[2]
+        force_rows = lax.axis_size("blk") * aic.shape[0]
+        if force_rows <= 2 * node_modes.shape[2]:
+            return by_collectives(*operands)
+        return by_rotation(*operands)
+
     return jax.shard_map(
         shards, mesh=mesh, in_specs=placed, out_specs=P("groups", None), check_vma=False
     )

time: 331 us -> 178 us (0.54)
  waiting for transfers between devices: 196 us -> 90.3 us
  starting transfers between devices: 77.9 us -> 6.48 us
  blocking collectives: 21.2 us -> 56.2 us
  matrix products: 16 us -> 5.4 us
    ppermute x3 -> x0, waiting for transfers between devices: 100 us -> none  [shifted(): return lax.ppermute(value, axis, pairs)]
    all_to_all x2 -> x1, starting transfers between devices: 72.7 us -> 6.48 us  [by_collectives(): mine = lax.all_to_all(aic, 'blk', split_axis=1, concat_axis=0, tiled=True)]
    all_gather x4 -> x2, blocking collectives: 21.2 us -> 56.2 us  [the longest x1 39.9 us: by_collectives(): spline = lax.all_gather(spline, ('blk', 'col'), axis=0, tiled=True)]
    dot_general x6 -> x4, matrix products: 16 us -> 5.4 us  [the longest x1 3.43 us: by_collectives(): jnp.dot(mine, downwash[0], precision=HIGHEST, preferred_element_type=jnp....]
    ppermute x3 -> x0, starting transfers between devices: 5.08 us -> none  [shifted(): return lax.ppermute(value, axis, pairs)]
    all_to_all x2 -> x1, waiting for transfers between devices: 4.72 us -> 0.01 us  [by_collectives(): mine = lax.all_to_all(aic, 'blk', split_axis=1, concat_axis=0, tiled=True)]
  transfers between devices with their start and end apart: 6 -> 2, of which waited for: 4 -> 1; matrix products, arithmetic and copies ran while one was open for 6% -> 1% of each run, Pallas kernels for 0% -> 0%
where the time goes in v1:
time: 178 us
  waiting for transfers between devices  90.3 us (51%)
  blocking collectives  56.2 us (32%)
  between operations  13.5 us (8%)
  starting transfers between devices  6.48 us (4%)
  local copies, waits for them, and re-layouts  5.88 us (3%)
  matrix products  5.4 us (3%)
    psum x1, waiting for transfers between devices, by_collectives(): return lax.psum(part, ('blk', 'col'))  90.2 us
    all_gather x1, blocking collectives, by_collectives(): spline = lax.all_gather(spline, ('blk', 'col'), axis=0, tiled=True)  39.9 us
    all_gather x1, blocking collectives, by_collectives(): every_mode = lax.all_gather(node_modes, 'blk', axis=1, tiled=True)  16.3 us
    all_to_all x1, starting transfers between devices, by_collectives(): mine = lax.all_to_all(aic, 'blk', split_axis=1, concat_axis=0, tiled=True)  6.48 us
  transfers between devices with their start and end apart: 2, of which 1 were waited for; matrix products, arithmetic and copies ran while one was open for 1% of the time, Pallas kernels for 0%

profile of v1, /device:TPU:0, one launch (start us, length us, event | category | flops | bytes accessed | tf_op | source)
XLA Modules:
  0.0 177.7 jit_solution(15378610462138258869)
XLA Ops:
  6.5 0.0 copy-start
  6.5 0.0 copy-start.2
  6.5 2.5 %copy.21 = f32[4,4,8,2048]{3,2,0,1:T(8,128)} copy(f32[4,4,8,2048]{3,2,1,0:T(8,128)} %bitcast.29) | data formatting | bytes 2097152 | tf_op jit(solution)/shard_map/all_to_all | solution.py:87
  9.0 6.5 %all-to-all-start = ((f32[32,4,2048]{2,0,1:T(8,128)}), f32[32,4,2048]{2,0,1:T(8,128)}, u32[]{:S(2)}, u32[]{:S(2)}) async-start(f32[32,4,2048]{2,0,1:T(8,128)} %bitcast.28), calls=%async_computation | async-start | bytes 2097152 | tf_op jit(solution)/shard_map/all_to_all | solution.py:87
  15.5 0.0 all-reduce.2.cloned.1.call-start
  15.5 0.0 copy-done.2
  15.5 0.0 copy-done.5
  15.5 0.1 iota_compare_fusion.3
  15.6 0.0 copy-done.4
  15.6 0.0 copy-done.3
  15.6 0.3 convolution_bitcast_fusion
  15.9 0.1 copy.15
  16.0 39.9 %all_gather.6 = f32[128,6,4,8]{3,2,1,0:T(4,128)} all-gather(f32[8,6,4,8]{3,2,1,0:T(4,128)S(1)} %copy.15), channel_id=1, replica_groups=mesh['groups'=2,'blk'=4,'col'=4] {'blk','col'}, dimensions={0}, use_global_device_ids=true | all-gather | bytes 104448 | tf_op jit(solution)/shard_map/all_gather | solution.py:94
  55.9 1.6 copy.16
  57.5 0.0 copy-done.1
  57.5 16.3 %all_gather.7 = f32[6,32,192]{2,1,0:T(8,128)S(1)} all-gather(f32[6,8,192]{2,1,0:T(8,128)S(1)} %copy-done.1), channel_id=1, replica_groups=mesh['groups'=2,'blk'=4,'col'=4] {'blk'}, dimensions={1}, use_global_device_ids=true | all-gather | bytes 184320 | tf_op jit(solution)/shard_map/all_gather | solution.py:95
  73.8 0.6 fusion.13
  74.4 0.0 all-to-all-done
  74.4 0.0 copy-done
  74.4 3.4 %fusion = f32[128,384]{1,0:T(8,128)S(1)} fusion(f32[128,2048]{1,0:T(8,128)} %bitcast.10, f32[1,2048,384]{2,1,0:T(8,128)S(1)} %copy-done), kind=kOutput, calls=%fused_computation | convolution fusion | flops 1207959552 | bytes 4390912 | tf_op jit(solution)/shard_map/dot_general | solution.py:101
  77.8 1.1 fusion.14
  78.9 0.0 all-reduce.2.cloned.1.call-update
  79.0 90.2 %all-reduce.2.cloned.1.call-done = f32[192,384]{1,0:T(8,128)} async-done(((f32[192,384]{1,0:T(8,128)}), f32[192,384]{1,0:T(8,128)}) %all-reduce.2.cloned.1.call-update) | async-done | bytes 294928 | tf_op jit(solution)/shard_map/psum | solution.py:103
  169.2 1.7 copy.23
  (6 shorter events, 0.0 us)
Async XLA Ops:
  6.5 67.9 %copy-start = (f32[1,2048,384]{2,1,0:T(8,128)S(1)}, f32[1,2048,384]{2,1,0:T(8,128)}, u32[]{:S(2)}) copy-start(f32[1,2048,384]{2,1,0:T(8,128)} %param.8) | copy-start | bytes 9437188
  6.5 8.9 %copy-start.2 = (f32[1,1,6,4,8]{4,3,2,1,0:T(4,128)S(1)}, f32[1,1,6,4,8]{4,3,2,1,0:T(4,128)}, u32[]{:S(2)}) copy-start(f32[1,1,6,4,8]{4,3,2,1,0:T(4,128)} %param.13) | copy-start | bytes 2308
  6.5 9.0 %copy-start.5 = (s32[1,1,4]{2,1,0:T(1,128)S(1)}, s32[1,1,4]{2,1,0:T(1,128)}, u32[]{:S(2)}) copy-start(s32[1,1,4]{2,1,0:T(1,128)} %param.12) | copy-start | bytes 52
  6.5 9.0 %copy-start.4 = (s32[1,1,4,8]{3,2,1,0:T(4,128)S(1)}, s32[1,1,4,8]{3,2,1,0:T(4,128)}, u32[]{:S(2)}) copy-start(s32[1,1,4,8]{3,2,1,0:T(4,128)} %param.11) | copy-start | bytes 388
  6.5 9.0 %copy-start.3 = (s32[1,1,4,8]{3,2,1,0:T(4,128)S(1)}, s32[1,1,4,8]{3,2,1,0:T(4,128)}, u32[]{:S(2)}) copy-start(s32[1,1,4,8]{3,2,1,0:T(4,128)} %param.10) | copy-start | bytes 388
  9.0 48.5 %copy-start.1 = (f32[6,8,192]{2,1,0:T(8,128)S(1)}, f32[6,8,192]{2,1,0:T(8,128)}, u32[]{:S(2)}) copy-start(f32[6,8,192]{2,1,0:T(8,128)} %param.9) | copy-start | bytes 110596
  9.0 65.4 %all-to-all-start = ((f32[32,4,2048]{2,0,1:T(8,128)}), f32[32,4,2048]{2,0,1:T(8,128)}, u32[]{:S(2)}, u32[]{:S(2)}) async-start(f32[32,4,2048]{2,0,1:T(8,128)} %bitcast.28), calls=%async_computation | async-start | bytes 2097152 | tf_op jit(solution)/shard_map/all_to_all | solution.py:87
  15.5 153.7 %all-reduce.2.cloned.1.call-start = ((), (), s32[]{:S(2)}) async-start(), calls=%async_computation.1 | async-start | bytes 589824 | tf_op jit(solution)/shard_map/psum | solution.py:103
Sparse Core Ops, SparseCore 0:
  79.1 90.0 all-reduce.1

commit v2 on v0

--- a/solution.py
+++ b/solution.py
@@ -1,7 +1,14 @@
+import functools
+
 import jax
 import jax.numpy as jnp
 from jax import lax
+from jax.experimental import pallas as pl
+from jax.experimental.pallas import tpu as pltpu
 from jax.sharding import PartitionSpec as P
+
+
+HIGHEST = lax.Precision.HIGHEST
 
 
 def shifted(value, axis, steps):
@@ -10,7 +17,7 @@
     return lax.ppermute(value, axis, pairs)
 
 
-def shards(aic, downwash, node_modes, src_rows, dst_nodes, counts, spline_weights):
+def by_rotation(aic, downwash, node_modes, src_rows, dst_nodes, counts, spline_weights):
     cycle_size = lax.axis_size("blk")
     col_count = lax.axis_size("col")
     device = lax.axis_index("blk")
@@ -74,6 +81,392 @@
     return lax.psum(modal, ("blk", "col"))
 
 
+def split(value):
+    high = value.astype(jnp.bfloat16)
+    low = (value - high.astype(jnp.float32)).astype(jnp.bfloat16)
+    return high, low
+
+
+def exchange_kernel(
+    blocks,
+    cols,
+    aic,
+    panels,
+    node_modes,
+    rows_list,
+    nodes_list,
+    counts,
+    weights,
+    out,
+    influence,
+    shapes,
+    shapes_high,
+    shapes_low,
+    partial,
+    plane_in,
+    line_in,
+    pressure,
+    spline,
+    mode_rows,
+    force,
+    local_sem,
+    aic_send,
+    aic_recv,
+    plane_send,
+    plane_recv,
+    line_send,
+    line_recv,
+    final_send,
+    final_recv,
+    spline_send,
+    spline_recv,
+    mode_send,
+    mode_recv,
+):
+    b = lax.axis_index("blk")
+    c = lax.axis_index("col")
+    chunks, _, sub, depth = influence.shape
+    dofs, _, node_count, modes = mode_rows.shape
+    owners, slots = rows_list.shape[2:]
+    width = panels.shape[2]
+    senders = min(cols, dofs)
+    while dofs % senders:
+        senders -= 1
+    share = dofs // senders
+    pieces = local_sem.shape[0] - chunks - 1
+    piece = depth // pieces
+
+    def on_line(k):
+        return lax.rem(b + k, blocks)
+
+    def on_plane(k):
+        return lax.rem(c + k, cols)
+
+    def to_line(k, source, target, send, recv):
+        return pltpu.make_async_remote_copy(
+            src_ref=source,
+            dst_ref=target,
+            send_sem=send,
+            recv_sem=recv,
+            device_id={"blk": on_line(k)},
+            device_id_type=pl.DeviceIdType.MESH,
+        )
+
+    def to_plane(k, source, target, send, recv):
+        return pltpu.make_async_remote_copy(
+            src_ref=source,
+            dst_ref=target,
+            send_sem=send,
+            recv_sem=recv,
+            device_id={"col": on_plane(k)},
+            device_id_type=pl.DeviceIdType.MESH,
+        )
+
+    shape_copies = []
+    for p in range(pieces):
+        span = pl.ds(p * piece, piece)
+        shape_copies.append(
+            pltpu.make_async_copy(panels.at[0, span], shapes.at[span], local_sem.at[p])
+        )
+        shape_copies[-1].start()
+    own_copies = []
+    for q in range(chunks):
+        own_copies.append(
+            pltpu.make_async_copy(
+                aic.at[pl.ds(q * sub, sub), pl.ds(pl.multiple_of(b * depth, depth), depth)],
+                influence.at[q, b],
+                local_sem.at[pieces + q],
+            )
+        )
+        own_copies[-1].start()
+    dof_span = pl.ds(lax.rem(c, senders) * share, share)
+    own_modes = pltpu.make_async_copy(
+        node_modes.at[dof_span], mode_rows.at[dof_span, b], local_sem.at[pieces + chunks]
+    )
+
+    barrier = pltpu.get_barrier_semaphore()
+    for k in range(1, blocks):
+        pl.semaphore_signal(
+            barrier, inc=1, device_id={"blk": on_line(k)}, device_id_type=pl.DeviceIdType.MESH
+        )
+    for k in range(1, cols):
+        pl.semaphore_signal(
+            barrier, inc=1, device_id={"col": on_plane(k)}, device_id_type=pl.DeviceIdType.MESH
+        )
+    pl.semaphore_wait(barrier, blocks + cols - 2)
+
+    aic_out = {}
+
+    def send_rows(q):
+        for k in range(1, blocks):
+            peer = on_line(k)
+            copy = to_line(
+                k,
+                aic.at[pl.ds(q * sub, sub), pl.ds(pl.multiple_of(peer * depth, depth), depth)],
+                influence.at[q, b],
+                aic_send.at[q, k - 1],
+                aic_recv.at[q, k - 1],
+            )
+            copy.start()
+            aic_out[q, k] = copy
+
+    ahead = min(2, chunks)
+    for q in range(ahead):
+        send_rows(q)
+        if q == 0:
+            mode_out = [
+                to_line(
+                    k,
+                    node_modes.at[dof_span],
+                    mode_rows.at[dof_span, b],
+                    mode_send.at[k - 1],
+                    mode_recv.at[k - 1],
+                )
+                for k in range(1, blocks)
+            ]
+
+            @pl.when(c < senders)
+            def _():
+                own_modes.start()
+                for copy in mode_out:
+                    copy.start()
+
+            length = dofs * owners * node_count
+            row_at = lax.broadcasted_iota(jnp.int32, (sub, length), 0)
+            column_at = lax.broadcasted_iota(jnp.int32, (sub, length), 1)
+            total = jnp.zeros((sub, length), jnp.float32)
+            for o in range(owners):
+                for s in range(slots):
+                    live = s < counts[0, 0, o]
+                    row = jnp.where(live, rows_list[0, 0, o, s], -1)
+                    node = nodes_list[0, 0, o, s] + o * node_count
+                    spread = jnp.zeros((sub, length), jnp.float32)
+                    for d in range(dofs):
+                        spread = jnp.where(
+                            column_at == node + d * owners * node_count,
+                            weights[0, 0, d, o, s],
+                            spread,
+                        )
+                    total = total + jnp.where(row_at == row, spread, 0.0)
+            spline[c, b] = total
+            spline_out = []
+            for k in range(1, blocks):
+                copy = to_line(
+                    k,
+                    spline.at[c, b],
+                    spline.at[c, b],
+                    spline_send.at[k - 1],
+                    spline_recv.at[k - 1],
+                )
+                copy.start()
+                spline_out.append(copy)
+
+    for p in range(pieces):
+        shape_copies[p].wait()
+        span = pl.ds(p * piece, piece)
+        high, low = split(shapes[span])
+        shapes_high[span] = high
+        shapes_low[span] = low
+
+    for copy in spline_out:
+        copy.wait()
+    for k in range(1, cols):
+        copy = to_plane(
+            k,
+            spline.at[c],
+            spline.at[c],
+            spline_send.at[blocks - 2 + k],
+            spline_recv.at[blocks - 2 + k],
+        )
+        copy.start()
+        spline_out.append(copy)
+    mode_plane = [
+        to_plane(
+            k,
+            mode_rows.at[dof_span],
+            mode_rows.at[dof_span],
+            mode_send.at[blocks - 2 + k],
+            mode_recv.at[blocks - 2 + k],
+        )
+        for k in range(1, cols)
+    ]
+
+    @pl.when(c < senders)
+    def _():
+        own_modes.wait()
+        for copy in mode_out:
+            copy.wait()
+        for copy in mode_plane:
+            copy.start()
+
+    plane_out, line_out, final_out = {}, {}, {}
+
+    def await_rows(q):
+        own_copies[q].wait()
+        for k in range(1, blocks):
+            aic_out[q, k].wait_recv()
+
+    def multiply(q):
+        high, low = split(influence[q].reshape(blocks * sub, depth))
+        product = jnp.dot(
+            jnp.concatenate([high, low], axis=0),
+            shapes_high[...],
+            preferred_element_type=jnp.float32,
+        )
+        rest = jnp.dot(high, shapes_low[...], preferred_element_type=jnp.float32)
+        lines = blocks * sub
+        product = product[:lines] + (product[lines:] + rest)
+        partial[q] = product.reshape(blocks, sub, width)
+        for k in range(1, cols):
+            copy = to_plane(
+                k,
+                partial.at[q, on_plane(k)],
+                plane_in.at[q, k - 1],
+                plane_send.at[q, k - 1],
+                plane_recv.at[q, k - 1],
+            )
+            copy.start()
+            plane_out[q, k] = copy
+
+    def over_plane(q):
+        total = partial[q, c]
+        for k in range(1, cols):
+            plane_out[q, k].wait_recv()
+            total = total + plane_in[q, k - 1]
+        line_in[q, b] = total
+        for k in range(1, blocks):
+            copy = to_line(
+                k,
+                line_in.at[q, b],
+                line_in.at[q, b],
+                line_send.at[q, k - 1],
+                line_recv.at[q, k - 1],
+            )
+            copy.start()
+            line_out[q, k] = copy
+
+    def over_line(q):
+        for k in range(1, blocks):
+            line_out[q, k].wait_recv()
+        total = line_in[q, 0]
+        for source in range(1, blocks):
+            total = total + line_in[q, source]
+        pressure[q, c] = total
+        for k in range(1, cols):
+            copy = to_plane(
+                k,
+                pressure.at[q, c],
+                pressure.at[q, c],
+                final_send.at[q, k - 1],
+                final_recv.at[q, k - 1],
+            )
+            copy.start()
+            final_out[q, k] = copy
+
+    def make_force():
+        for k in range(1, cols):
+            spline_out[blocks - 2 + k].wait_recv()
+
+            @pl.when(lax.rem(c + cols - k, cols) < senders)
+            def _():
+                mode_plane[k - 1].wait_recv()
+
+        length = dofs * owners * node_count
+        force[...] = jnp.dot(
+            spline[...].reshape(cols * blocks * sub, length),
+            mode_rows[...].reshape(length, modes),
+            precision=HIGHEST,
+            preferred_element_type=jnp.float32,
+        )
+
+    for q in range(chunks):
+        await_rows(q)
+        if q >= 1:
+            over_plane(q - 1)
+        if q + ahead < chunks:
+            send_rows(q + ahead)
+        multiply(q)
+        if q == 0:
+            make_force()
+        if q >= 2:
+            over_line(q - 2)
+    if chunks >= 2:
+        over_line(chunks - 2)
+    over_plane(chunks - 1)
+    over_line(chunks - 1)
+    for q in range(chunks):
+        for k in range(1, cols):
+            final_out[q, k].wait_recv()
+    out[...] = lax.dot_general(
+        force[...],
+        pressure[...].reshape(chunks * blocks * sub, width),
+        (((0,), (0,)), ((), ())),
+        precision=HIGHEST,
+        preferred_element_type=jnp.float32,
+    )
+
+    for copy in spline_out[blocks - 1 :]:
+        copy.wait_send()
+    for group in (aic_out, plane_out, line_out, final_out):
+        for copy in group.values():
+            copy.wait_send()
+
+    @pl.when(c < senders)
+    def _():
+        for copy in mode_plane:
+            copy.wait_send()
+
+
+def by_kernel(aic, downwash, node_modes, src_rows, dst_nodes, counts, spline_weights):
+    blocks = lax.axis_size("blk")
+    cols = lax.axis_size("col")
+    rows = aic.shape[0]
+    sub = rows // cols
+    depth, width = downwash.shape[1:]
+    dofs, node_count, modes = node_modes.shape
+    length = dofs * blocks * node_count
+    pieces = 4
+    dma = pltpu.SemaphoreType.DMA
+    anywhere = pl.BlockSpec(memory_space=pl.ANY)
+    scalars = pl.BlockSpec(memory_space=pltpu.SMEM)
+    return pl.pallas_call(
+        functools.partial(exchange_kernel, blocks, cols),
+        name="gaf_exchange",
+        out_shape=jax.ShapeDtypeStruct((modes, width), jnp.float32),
+        in_specs=[anywhere, anywhere, anywhere, scalars, scalars, scalars, scalars],
+        out_specs=pl.BlockSpec(memory_space=pltpu.VMEM),
+        scratch_shapes=[
+            pltpu.VMEM((cols, blocks, sub, depth), jnp.float32),
+            pltpu.VMEM((depth, width), jnp.float32),
+            pltpu.VMEM((depth, width), jnp.bfloat16),
+            pltpu.VMEM((depth, width), jnp.bfloat16),
+            pltpu.VMEM((cols, blocks, sub, width), jnp.float32),
+            pltpu.VMEM((cols, cols - 1, sub, width), jnp.float32),
+            pltpu.VMEM((cols, blocks, sub, width), jnp.float32),
+            pltpu.VMEM((cols, blocks, sub, width), jnp.float32),
+            pltpu.VMEM((cols, blocks, sub, length), jnp.float32),
+            pltpu.VMEM((dofs, blocks, node_count, modes), jnp.float32),
+            pltpu.VMEM((cols * blocks * sub, modes), jnp.float32),
+            dma((pieces + cols + 1,)),
+            dma((cols, blocks - 1)),
+            dma((cols, blocks - 1)),
+            dma((cols, cols - 1)),
+            dma((cols, cols - 1)),
+            dma((cols, blocks - 1)),
+            dma((cols, blocks - 1)),
+            dma((cols, cols - 1)),
+            dma((cols, cols - 1)),
+            dma((blocks + cols - 2,)),
+            dma((blocks + cols - 2,)),
+            dma((blocks + cols - 2,)),
+            dma((blocks + cols - 2,)),
+        ],
+        compiler_params=pltpu.CompilerParams(
+            collective_id=0, has_side_effects=True, vmem_limit_bytes=60 * 1024 * 1024
+        ),
+    )(aic, downwash, node_modes, src_rows, dst_nodes, counts, spline_weights)
+
+
 def solution(mesh):
     placed = (
         P(("groups", "blk"), "col"),
@@ -84,6 +477,16 @@
         P("blk", "col", None),
         P("blk", "col", None, None, None),
     )
+
+    def shards(*operands):
+        aic, downwash, node_modes = operands[:3]
+        blocks, cols = lax.axis_size("blk"), lax.axis_size("col")
+        small = blocks * aic.shape[0] <= 2 * node_modes.shape[2]
+        even = blocks == cols and aic.shape[0] % (8 * cols) == 0 and downwash.shape[1] % 512 == 0
+        if small and even:
+            return by_kernel(*operands)
+        return by_rotation(*operands)
+
     return jax.shard_map(
         shards, mesh=mesh, in_specs=placed, out_specs=P("groups", None), check_vma=False
     )

time: 331 us -> 48.4 us (0.15)
  waiting for transfers between devices: 196 us -> 0 us
  starting transfers between devices: 77.9 us -> 0 us
  Pallas kernels: 0 us -> 46.4 us
  blocking collectives: 21.2 us -> 0 us
  matrix products: 16 us -> 0 us
  between operations: 13.6 us -> 0.01 us
  local copies, waits for them, and re-layouts: 5.54 us -> 1.69 us
    ppermute x3 -> x0, waiting for transfers between devices: 100 us -> none  [shifted(): return lax.ppermute(value, axis, pairs)]
    psum x1 -> x0, waiting for transfers between devices: 90.9 us -> none  [shards(): return lax.psum(modal, ('blk', 'col'))]
    all_to_all x2 -> x0, starting transfers between devices: 72.7 us -> none  [the longest x1 69.4 us: shards(): lax.all_to_all(spread, 'blk', split_axis=1, concat_axis=1, tiled=True)]
    pallas_call x0 -> x1, Pallas kernels: none -> 46.4 us  [by_kernel(): pl.pallas_call(functools.partial(exchange_kernel, blocks, cols), name='ga...]
    all_gather x4 -> x0, blocking collectives: 21.2 us -> none  [the longest x1 5.42 us: shards(): weight_all = lax.all_gather(spline_weights, 'col', axis=1, tiled=True)]
    dot_general x6 -> x0, matrix products: 16 us -> none  [the longest x4 14.6 us: product(): jnp.dot(columns, shapes, precision=lax.Precision.HIGHEST, preferred_eleme...]
    ppermute x3 -> x0, starting transfers between devices: 5.08 us -> none  [shifted(): return lax.ppermute(value, axis, pairs)]
    all_to_all x2 -> x0, waiting for transfers between devices: 4.72 us -> none  [the longest x1 4.72 us: shards(): lax.all_to_all(forces, 'blk', split_axis=1, concat_axis=1, tiled=True)]
  transfers between devices with their start and end apart: 6 -> 0, of which waited for: 4 -> 0; matrix products, arithmetic and copies ran while one was open for 6% -> 0% of each run, Pallas kernels for 0% -> 0%
where the time goes in v2:
time: 48.4 us; the launch traced here: 48.1 us
  Pallas kernels  46.4 us (96%)
  local copies, waits for them, and re-layouts  1.69 us (3%)
    pallas_call x1, Pallas kernels, by_kernel(): pl.pallas_call(functools.partial(exchange_kernel, blocks, cols), name='ga...  46.4 us
    unnamed x1, local copies, waits for them, and re-layouts  1.69 us

profile of v2, /device:TPU:0, one launch (start us, length us, event | category | flops | bytes accessed | tf_op | source)
XLA Modules:
  0.0 48.1 jit_solution(5163968758849908545)
XLA Ops:
  0.0 46.4 %gaf_exchange.1 = f32[192,384]{1,0:T(8,128)} custom-call(f32[32,8192]{1,0:T(8,128)} %aic.1, f32[1,2048,384]{2,1,0:T(8,128)} %panels.1, f32[6,8,192]{2,1,0:T(8,128)} %node_modes.1, s32[1,1,4,8]{3,2,1,0:T(4,128)} %rows_list.1, s32[1,1,4,8]{3,2,1,0:T(4,128)} %nodes_list.1, s32[1,1,4]{2,1,0:T(1,128)} %counts.1, f32[1,1,6,4,8]{4,3,2,1,0:T(4,128)} %weights.1), custom_call_target="tpu_custom_call" | custom-call | tf_op jit(solution)/shard_map/gaf_exchange/pallas_call | solution.py:432
  46.4 1.7 %copy.9 = f32[192,384]{1,0:T(8,128)} copy(f32[192,384]{1,0:T(8,128)} %gaf_exchange.1) | data formatting | bytes 589824

commit v3 on v2

--- a/solution.py
+++ b/solution.py
@@ -93,10 +93,10 @@
     aic,
     panels,
     node_modes,
-    rows_list,
-    nodes_list,
-    counts,
-    weights,
+    rows_hbm,
+    nodes_hbm,
+    counts_hbm,
+    weights_hbm,
     out,
     influence,
     shapes,
@@ -109,6 +109,11 @@
     spline,
     mode_rows,
     force,
+    rows_list,
+    nodes_list,
+    counts,
+    weights,
+    list_sem,
     local_sem,
     aic_send,
     aic_recv,
@@ -162,6 +167,11 @@
             device_id_type=pl.DeviceIdType.MESH,
         )
 
+    list_copies = []
+    lists = ((rows_hbm, rows_list), (nodes_hbm, nodes_list), (counts_hbm, counts), (weights_hbm, weights))
+    for i, (source, target) in enumerate(lists):
+        list_copies.append(pltpu.make_async_copy(source, target, list_sem.at[i]))
+        list_copies[-1].start()
     shape_copies = []
     for p in range(pieces):
         span = pl.ds(p * piece, piece)
@@ -235,6 +245,8 @@
             row_at = lax.broadcasted_iota(jnp.int32, (sub, length), 0)
             column_at = lax.broadcasted_iota(jnp.int32, (sub, length), 1)
             total = jnp.zeros((sub, length), jnp.float32)
+            for copy in list_copies:
+                copy.wait()
             for o in range(owners):
                 for s in range(slots):
                     live = s < counts[0, 0, o]
@@ -379,31 +391,41 @@
             preferred_element_type=jnp.float32,
         )
 
+    def modal(start, stop):
+        force_rows = force[pl.ds(start * blocks * sub, (stop - start) * blocks * sub)]
+        return lax.dot_general(
+            force_rows,
+            pressure[start:stop].reshape((stop - start) * blocks * sub, width),
+            (((0,), (0,)), ((), ())),
+            precision=HIGHEST,
+            preferred_element_type=jnp.float32,
+        )
+
+    def await_pressure(q):
+        for k in range(1, cols):
+            final_out[q, k].wait_recv()
+
     for q in range(chunks):
         await_rows(q)
-        if q >= 1:
-            over_plane(q - 1)
+        multiply(q)
+        over_plane(q)
         if q + ahead < chunks:
             send_rows(q + ahead)
-        multiply(q)
         if q == 0:
             make_force()
-        if q >= 2:
-            over_line(q - 2)
-    if chunks >= 2:
-        over_line(chunks - 2)
-    over_plane(chunks - 1)
-    over_line(chunks - 1)
-    for q in range(chunks):
-        for k in range(1, cols):
-            final_out[q, k].wait_recv()
-    out[...] = lax.dot_general(
-        force[...],
-        pressure[...].reshape(chunks * blocks * sub, width),
-        (((0,), (0,)), ((), ())),
-        precision=HIGHEST,
-        preferred_element_type=jnp.float32,
-    )
+        else:
+            over_line(q - 1)
+    last = chunks - 1
+    over_line(last)
+    if last:
+        for q in range(last):
+            await_pressure(q)
+        out[...] = modal(0, last)
+        await_pressure(last)
+        out[...] += modal(last, chunks)
+    else:
+        await_pressure(last)
+        out[...] = modal(last, chunks)
 
     for copy in spline_out[blocks - 1 :]:
         copy.wait_send()
@@ -428,12 +450,11 @@
     pieces = 4
     dma = pltpu.SemaphoreType.DMA
     anywhere = pl.BlockSpec(memory_space=pl.ANY)
-    scalars = pl.BlockSpec(memory_space=pltpu.SMEM)
     return pl.pallas_call(
         functools.partial(exchange_kernel, blocks, cols),
         name="gaf_exchange",
         out_shape=jax.ShapeDtypeStruct((modes, width), jnp.float32),
-        in_specs=[anywhere, anywhere, anywhere, scalars, scalars, scalars, scalars],
+        in_specs=[anywhere] * 7,
         out_specs=pl.BlockSpec(memory_space=pltpu.VMEM),
         scratch_shapes=[
             pltpu.VMEM((cols, blocks, sub, depth), jnp.float32),
@@ -447,6 +468,11 @@
             pltpu.VMEM((cols, blocks, sub, length), jnp.float32),
             pltpu.VMEM((dofs, blocks, node_count, modes), jnp.float32),
             pltpu.VMEM((cols * blocks * sub, modes), jnp.float32),
+            pltpu.SMEM(src_rows.shape, jnp.int32),
+            pltpu.SMEM(dst_nodes.shape, jnp.int32),
+            pltpu.SMEM(counts.shape, jnp.int32),
+            pltpu.SMEM(spline_weights.shape, jnp.float32),
+            dma((4,)),
             dma((pieces + cols + 1,)),
             dma((cols, blocks - 1)),
             dma((cols, blocks - 1)),

time: 48.4 us -> 52.9 us (1.093)
  Pallas kernels: 46.4 us -> 51.1 us
    pallas_call x1, Pallas kernels: 46.4 us -> 51.1 us  [by_kernel(): pl.pallas_call(functools.partial(exchange_kernel, blocks, cols), name='ga...]
where the time goes in v3:
time: 52.9 us; the launch traced here: 52.8 us
  Pallas kernels  51.1 us (97%)
  local copies, waits for them, and re-layouts  1.69 us (3%)
    pallas_call x1, Pallas kernels, by_kernel(): pl.pallas_call(functools.partial(exchange_kernel, blocks, cols), name='ga...  51.1 us
    unnamed x1, local copies, waits for them, and re-layouts  1.69 us

profile of v3, /device:TPU:0, one launch (start us, length us, event | category | flops | bytes accessed | tf_op | source)
XLA Modules:
  0.0 52.8 jit_solution(13006173143700462565)
XLA Ops:
  0.0 51.1 %gaf_exchange.1 = f32[192,384]{1,0:T(8,128)} custom-call(f32[32,8192]{1,0:T(8,128)} %aic.1, f32[1,2048,384]{2,1,0:T(8,128)} %panels.1, f32[6,8,192]{2,1,0:T(8,128)} %node_modes.1, s32[1,1,4,8]{3,2,1,0:T(4,128)} %rows_hbm.1, s32[1,1,4,8]{3,2,1,0:T(4,128)} %nodes_hbm.1, s32[1,1,4]{2,1,0:T(1,128)} %counts_hbm.1, f32[1,1,6,4,8]{4,3,2,1,0:T(4,128)} %weights_hbm.1), custom_call_target="tpu_custom_call" | custom-call | tf_op jit(solution)/shard_map/gaf_exchange/pallas_call | solution.py:453
  51.1 1.7 %copy.9 = f32[192,384]{1,0:T(8,128)} copy(f32[192,384]{1,0:T(8,128)} %gaf_exchange.1) | data formatting | bytes 589824

commit v4 on v3

--- a/solution.py
+++ b/solution.py
@@ -220,7 +220,7 @@
             copy.start()
             aic_out[q, k] = copy
 
-    ahead = min(2, chunks)
+    ahead = min(4, chunks)
     for q in range(ahead):
         send_rows(q)
         if q == 0:
@@ -407,16 +407,18 @@
 
     for q in range(chunks):
         await_rows(q)
-        multiply(q)
-        over_plane(q)
         if q + ahead < chunks:
             send_rows(q + ahead)
-        if q == 0:
+        multiply(q)
+        if q == chunks - 1:
+            for earlier in range(q):
+                over_plane(earlier)
+        if q == 1:
             make_force()
-        else:
-            over_line(q - 1)
     last = chunks - 1
-    over_line(last)
+    over_plane(last)
+    for q in range(chunks):
+        over_line(q)
     if last:
         for q in range(last):
             await_pressure(q)

time: 52.9 us -> 45.4 us (0.86)
  Pallas kernels: 51.1 us -> 43.6 us
    pallas_call x1, Pallas kernels: 51.1 us -> 43.6 us  [by_kernel(): pl.pallas_call(functools.partial(exchange_kernel, blocks, cols), name='ga...]
where the time goes in v4:
time: 45.4 us; the launch traced here: 45.3 us
  Pallas kernels  43.6 us (96%)
  local copies, waits for them, and re-layouts  1.69 us (4%)
    pallas_call x1, Pallas kernels, by_kernel(): pl.pallas_call(functools.partial(exchange_kernel, blocks, cols), name='ga...  43.6 us
    unnamed x1, local copies, waits for them, and re-layouts  1.69 us

profile of v4, /device:TPU:0, one launch (start us, length us, event | category | flops | bytes accessed | tf_op | source)
XLA Modules:
  0.0 45.3 jit_solution(2808780791326669564)
XLA Ops:
  0.0 43.6 %gaf_exchange.1 = f32[192,384]{1,0:T(8,128)} custom-call(f32[32,8192]{1,0:T(8,128)} %aic.1, f32[1,2048,384]{2,1,0:T(8,128)} %panels.1, f32[6,8,192]{2,1,0:T(8,128)} %node_modes.1, s32[1,1,4,8]{3,2,1,0:T(4,128)} %rows_hbm.1, s32[1,1,4,8]{3,2,1,0:T(4,128)} %nodes_hbm.1, s32[1,1,4]{2,1,0:T(1,128)} %counts_hbm.1, f32[1,1,6,4,8]{4,3,2,1,0:T(4,128)} %weights_hbm.1), custom_call_target="tpu_custom_call" | custom-call | tf_op jit(solution)/shard_map/gaf_exchange/pallas_call | solution.py:455
  43.6 1.7 %copy.9 = f32[192,384]{1,0:T(8,128)} copy(f32[192,384]{1,0:T(8,128)} %gaf_exchange.1) | data formatting | bytes 589824

commit v5 on v4

--- a/solution.py
+++ b/solution.py
@@ -490,7 +490,7 @@
             dma((blocks + cols - 2,)),
         ],
         compiler_params=pltpu.CompilerParams(
-            collective_id=0, has_side_effects=True, vmem_limit_bytes=60 * 1024 * 1024
+            collective_id=0, has_side_effects=True, vmem_limit_bytes=54200 * 1024
         ),
     )(aic, downwash, node_modes, src_rows, dst_nodes, counts, spline_weights)
 

time: 45.4 us -> 47.3 us (1.042)
  local copies, waits for them, and re-layouts: 1.69 us -> 4.24 us
  Pallas kernels: 43.6 us -> 42.8 us
    unnamed x1 -> x11, local copies, waits for them, and re-layouts: 1.69 us -> 4.24 us
    pallas_call x1, Pallas kernels: 43.6 us -> 42.8 us  [by_kernel(): pl.pallas_call(functools.partial(exchange_kernel, blocks, cols), name='ga...]
where the time goes in v5:
time: 47.3 us; the launch traced here: 47.1 us
  Pallas kernels  42.8 us (90%)
  local copies, waits for them, and re-layouts  4.24 us (9%)
    pallas_call x1, Pallas kernels, by_kernel(): pl.pallas_call(functools.partial(exchange_kernel, blocks, cols), name='ga...  42.8 us
    unnamed x11, local copies, waits for them, and re-layouts  4.24 us

profile of v5, /device:TPU:0, one launch (start us, length us, event | category | flops | bytes accessed | tf_op | source)
XLA Modules:
  0.0 47.1 jit_solution(3171928829923956338)
XLA Ops:
  0.0 0.0 copy-start
  0.0 0.8 %copy-done = f32[6,8,192]{2,1,0:T(8,128)S(1)} copy-done((f32[6,8,192]{2,1,0:T(8,128)S(1)}, f32[6,8,192]{2,1,0:T(8,128)}, u32[]{:S(2)}) %copy-start) | copy-done | bytes 36888
  0.8 0.0 copy-start.1
  0.8 0.7 %copy-done.1 = f32[1,1,6,4,8]{4,3,2,1,0:T(4,128)S(1)} copy-done((f32[1,1,6,4,8]{4,3,2,1,0:T(4,128)S(1)}, f32[1,1,6,4,8]{4,3,2,1,0:T(4,128)}, u32[]{:S(2)}) %copy-start.1) | copy-done | bytes 792
  1.5 0.0 copy-start.2
  1.5 0.7 %copy-done.2 = s32[1,1,4,8]{3,2,1,0:T(4,128)S(1)} copy-done((s32[1,1,4,8]{3,2,1,0:T(4,128)S(1)}, s32[1,1,4,8]{3,2,1,0:T(4,128)}, u32[]{:S(2)}) %copy-start.2) | copy-done | bytes 152
  2.2 0.0 copy-start.3
  2.2 0.7 %copy-done.3 = s32[1,1,4,8]{3,2,1,0:T(4,128)S(1)} copy-done((s32[1,1,4,8]{3,2,1,0:T(4,128)S(1)}, s32[1,1,4,8]{3,2,1,0:T(4,128)}, u32[]{:S(2)}) %copy-start.3) | copy-done | bytes 152
  2.9 0.0 copy-start.4
  2.9 0.7 %copy-done.4 = s32[1,1,4]{2,1,0:T(1,128)S(1)} copy-done((s32[1,1,4]{2,1,0:T(1,128)S(1)}, s32[1,1,4]{2,1,0:T(1,128)}, u32[]{:S(2)}) %copy-start.4) | copy-done | bytes 40
  3.5 42.8 %gaf_exchange.1 = f32[192,384]{1,0:T(8,128)S(1)} custom-call(f32[32,8192]{1,0:T(8,128)} %aic.1, f32[1,2048,384]{2,1,0:T(8,128)} %panels.1, f32[6,8,192]{2,1,0:T(8,128)S(1)} %copy-done, s32[1,1,4,8]{3,2,1,0:T(4,128)S(1)} %copy-done.2, s32[1,1,4,8]{3,2,1,0:T(4,128)S(1)} %copy-done.3, s32[1,1,4]{2,1,0:T(1,128)S(1)} %copy-done.4, f32[1,1,6,4,8]{4,3,2,1,0:T(4,128)S(1)} %copy-done.1), custom_call_target="tpu_custom_call" | custom-call | tf_op jit(solution)/shard_map/gaf_exchange/pallas_call | solution.py:455
  46.4 0.7 %copy.9 = f32[192,384]{1,0:T(8,128)} copy(f32[192,384]{1,0:T(8,128)S(1)} %gaf_exchange.1) | data formatting | bytes 589824
Async XLA Ops:
  0.0 0.8 %copy-start = (f32[6,8,192]{2,1,0:T(8,128)S(1)}, f32[6,8,192]{2,1,0:T(8,128)}, u32[]{:S(2)}) copy-start(f32[6,8,192]{2,1,0:T(8,128)} %node_modes.1) | copy-start | bytes 110596
  0.8 0.7 %copy-start.1 = (f32[1,1,6,4,8]{4,3,2,1,0:T(4,128)S(1)}, f32[1,1,6,4,8]{4,3,2,1,0:T(4,128)}, u32[]{:S(2)}) copy-start(f32[1,1,6,4,8]{4,3,2,1,0:T(4,128)} %weights_hbm.1) | copy-start | bytes 2308
  1.5 0.7 %copy-start.2 = (s32[1,1,4,8]{3,2,1,0:T(4,128)S(1)}, s32[1,1,4,8]{3,2,1,0:T(4,128)}, u32[]{:S(2)}) copy-start(s32[1,1,4,8]{3,2,1,0:T(4,128)} %rows_hbm.1) | copy-start | bytes 388
  2.2 0.7 %copy-start.3 = (s32[1,1,4,8]{3,2,1,0:T(4,128)S(1)}, s32[1,1,4,8]{3,2,1,0:T(4,128)}, u32[]{:S(2)}) copy-start(s32[1,1,4,8]{3,2,1,0:T(4,128)} %nodes_hbm.1) | copy-start | bytes 388
  2.9 0.7 %copy-start.4 = (s32[1,1,4]{2,1,0:T(1,128)S(1)}, s32[1,1,4]{2,1,0:T(1,128)}, u32[]{:S(2)}) copy-start(s32[1,1,4]{2,1,0:T(1,128)} %counts_hbm.1) | copy-start | bytes 52
